TPU v7x, 32 devices: a whole 2x2x4 slice. The times are simulated.
32 devices in a mesh: fsdp: 32 (over z, y, x, core).
Axes of the slice: x: 2, y: 2, z: 4, core: 2. Of those that a mesh axis runs over, the one named last changes fastest.
Arguments:
- tokens: bfloat16 [512, 64, 768], P('fsdp'), may hold values from -6 to 6
- lengths: int32 [512], P('fsdp'), may hold values from 3 to 64, as said below
- partners: int32 [256], P('fsdp'), may hold values from 0 to 255, each once
- out_cotangent: bfloat16 [512, 64, 768], P('fsdp'), may hold values from -6 to 6
- w_query: bfloat16 [768, 768], P('fsdp'), may hold values from -0.21875 to 0.21875
- w_key: bfloat16 [768, 768], P('fsdp'), may hold values from -0.21875 to 0.21875
- w_value: bfloat16 [768, 768], P('fsdp'), may hold values from -0.21875 to 0.21875
- w_output: bfloat16 [768, 768], P('fsdp'), may hold values from -0.625 to 0.625
- b_query: bfloat16 [768], P('fsdp'), may hold values from -1.5 to 1.5
- b_value: bfloat16 [768], P('fsdp'), may hold values from -1.5 to 1.5
- b_output: bfloat16 [768], P('fsdp'), may hold values from -1.5 to 1.5
- gain_attn: bfloat16 [768], P('fsdp'), may hold values from 0.5 to 1.5
- shift_attn: bfloat16 [768], P('fsdp'), may hold values from -1.5 to 1.5
- w_inner: bfloat16 [768, 3072], P('fsdp'), may hold values from -0.21875 to 0.21875
- b_inner: bfloat16 [3072], P('fsdp'), may hold values from -1.5 to 1.5
- w_outer: bfloat16 [3072, 768], P('fsdp'), may hold values from -0.15625 to 0.15625
- b_outer: bfloat16 [768], P('fsdp'), may hold values from -1.5 to 1.5
- gain_ffn: bfloat16 [768], P('fsdp'), may hold values from 0.5 to 1.5
- shift_ffn: bfloat16 [768], P('fsdp'), may hold values from -1.5 to 1.5
Outputs:
- loss: float32 [], replicated
- block_out: bfloat16 [512, 64, 768], P('fsdp')
- grad_tokens: float32 [512, 64, 768], P('fsdp')
- grad_w_query: float32 [768, 768], P('fsdp')
- grad_w_key: float32 [768, 768], P('fsdp')
- grad_w_value: float32 [768, 768], P('fsdp')
- grad_w_output: float32 [768, 768], P('fsdp')
- grad_b_query: float32 [768], P('fsdp')
- grad_b_value: float32 [768], P('fsdp')
- grad_b_output: float32 [768], P('fsdp')
- grad_gain_attn: float32 [768], P('fsdp')
- grad_shift_attn: float32 [768], P('fsdp')
- grad_w_inner: float32 [768, 3072], P('fsdp')
- grad_b_inner: float32 [3072], P('fsdp')
- grad_w_outer: float32 [3072, 768], P('fsdp')
- grad_b_outer: float32 [768], P('fsdp')
- grad_gain_ffn: float32 [768], P('fsdp')
- grad_shift_ffn: float32 [768], P('fsdp')
Inputs may be any that keep to these rules, and one draw needn't show every extreme that they name: `lengths`: each sentence slot has 3 to 64 live tokens, heavy toward short ones; at least one slot has 64.
All inputs are finite; a program needn't handle non-finite values.
Results may differ from a plain program's by a relative error of at most 0.013.
Values may be sent and summed in bfloat16 or wider, within the bound.
No kernel may reach another device: no remote copies, remote signals or barrier semaphores. Data moves between devices by JAX's collectives and lax.ppermute only.
A program may use at most 192 MiB of HBM per device.

v0:
```python
import jax
import jax.numpy as jnp
from jax import lax
from jax.sharding import PartitionSpec as P

D = 768
HEADS = 12
HEAD_DIM = 64
LEN = 64
norm_eps = 1e-12
pool_eps = 1e-06
sim_scale = 50.0
sim_margin = 0.3


def project(rows, weight):
    return jnp.dot(rows, weight, preferred_element_type=jnp.float32)


def project_back(grad, weight):
    return lax.dot_general(
        grad, weight, (((1,), (1,)), ((), ())), preferred_element_type=jnp.float32
    )


def weight_grad(rows, grad):
    return lax.dot_general(rows, grad, (((0,), (0,)), ((), ())), preferred_element_type=jnp.float32)


def scaled_norm(field, gain_vec):
    centred = field - jnp.mean(field, axis=-1, keepdims=True)
    variance = jnp.mean(centred * centred, axis=-1, keepdims=True)
    return centred * lax.rsqrt(variance + norm_eps) * gain_vec


def exact_gelu(field):
    return jax.nn.gelu(field, approximate=False)


def normalize(field):
    return field * lax.rsqrt(jnp.sum(field * field, axis=-1, keepdims=True) + pool_eps)


def scores_of(queries, key_rows, visible):
    raw = jnp.einsum(
        "bqhd,bkhd->bhqk", queries, key_rows, preferred_element_type=jnp.float32
    ) * HEAD_DIM ** (-0.5)
    return jnp.where(visible, raw, -1e30)


def column_sum(field):
    return jnp.sum(field.astype(jnp.float32), axis=0)


def local(
    tokens,
    lengths,
    partners,
    out_cotangent,
    w_query,
    w_key,
    w_value,
    w_output,
    b_query,
    b_value,
    b_output,
    gain_attn,
    shift_attn,
    w_inner,
    b_inner,
    w_outer,
    b_outer,
    gain_ffn,
    shift_ffn,
):
    count = tokens.shape[0]
    half = count // 2
    shape_four = (count, LEN, HEADS, HEAD_DIM)
    token_rows = tokens.reshape(count * LEN, D)
    positions = jnp.arange(LEN, dtype=jnp.int32)
    visible = (positions[None, :] < lengths[:, None])[:, None, None, :]
    attn_full = (
        lax.all_gather(w_query, "fsdp", axis=0, tiled=True),
        lax.all_gather(w_key, "fsdp", axis=0, tiled=True),
        lax.all_gather(w_value, "fsdp", axis=0, tiled=True),
        lax.all_gather(w_output, "fsdp", axis=0, tiled=True),
        lax.all_gather(b_query, "fsdp", axis=0, tiled=True),
        lax.all_gather(b_value, "fsdp", axis=0, tiled=True),
        lax.all_gather(b_output, "fsdp", axis=0, tiled=True),
        lax.all_gather(gain_attn, "fsdp", axis=0, tiled=True),
        lax.all_gather(shift_attn, "fsdp", axis=0, tiled=True),
    )
    (
        query_mat,
        key_mat,
        value_mat,
        output_mat,
        query_bias,
        value_bias,
        output_bias,
        attn_gain,
        attn_shift,
    ) = attn_full
    queries = (project(token_rows, query_mat) + query_bias).astype(jnp.bfloat16).reshape(shape_four)
    key_rows = project(token_rows, key_mat).astype(jnp.bfloat16).reshape(shape_four)
    value_rows = (
        (project(token_rows, value_mat) + value_bias).astype(jnp.bfloat16).reshape(shape_four)
    )
    scores = scores_of(queries, key_rows, visible)
    row_top = jnp.max(scores, axis=-1, keepdims=True)
    expd = jnp.exp(scores - row_top)
    row_total = jnp.sum(expd, axis=-1, keepdims=True)
    probs = expd / row_total
    score_lse = row_top + jnp.log(row_total)
    context = jnp.einsum(
        "bhqk,bkhd->bqhd",
        probs.astype(jnp.bfloat16),
        value_rows,
        preferred_element_type=jnp.float32,
    )
    context = context.astype(jnp.bfloat16).reshape(count * LEN, D)
    resid_attn = token_rows.astype(jnp.float32) + (project(context, output_mat) + output_bias)
    normed_attn = scaled_norm(resid_attn, attn_gain.astype(jnp.float32)) + attn_shift
    ffn_full = (
        lax.all_gather(w_inner, "fsdp", axis=0, tiled=True),
        lax.all_gather(b_inner, "fsdp", axis=0, tiled=True),
        lax.all_gather(w_outer, "fsdp", axis=0, tiled=True),
        lax.all_gather(b_outer, "fsdp", axis=0, tiled=True),
        lax.all_gather(gain_ffn, "fsdp", axis=0, tiled=True),
        lax.all_gather(shift_ffn, "fsdp", axis=0, tiled=True),
    )
    inner_mat, inner_bias, outer_mat, outer_bias, ffn_gain, ffn_shift = ffn_full
    normed_low = normed_attn.astype(jnp.bfloat16)
    hidden_pre = project(normed_low, inner_mat) + inner_bias
    hidden_act = exact_gelu(hidden_pre).astype(jnp.bfloat16)
    resid_ffn = normed_attn + (project(hidden_act, outer_mat) + outer_bias)
    block_rows = scaled_norm(resid_ffn, ffn_gain.astype(jnp.float32)) + ffn_shift
    block_out = block_rows.astype(jnp.bfloat16).reshape(count, LEN, D)
    cls_rows = block_rows.reshape(count, LEN, D)[:, 0, :]
    unit, pool_back = jax.vjp(normalize, cls_rows)
    unit_low = unit.astype(jnp.bfloat16)
    every_unit = lax.all_gather(unit_low, "fsdp", axis=0, tiled=True)
    every_pair = every_unit.reshape(every_unit.shape[0] // 2, 2, D)
    all_targets = every_pair[:, 1, :]
    own_pair = unit_low.reshape(half, 2, D)
    own_sources = own_pair[:, 0, :]
    npairs = all_targets.shape[0]
    sims = project_back(own_sources, all_targets) * sim_scale
    matched = partners[:, None] == jnp.arange(npairs, dtype=jnp.int32)[None, :]
    sims = sims - jnp.where(matched, sim_scale * sim_margin, 0.0)
    sim_top = jnp.max(sims, axis=1, keepdims=True)
    row_lse = sim_top + jnp.log(jnp.sum(jnp.exp(sims - sim_top), axis=1, keepdims=True))
    col_part = jnp.sum(jnp.exp(sims - sim_scale), axis=0)
    positive = jnp.sum(jnp.where(matched, sims, 0.0))
    local_loss = jnp.sum(row_lse) - 2.0 * positive
    col_total, loss_total = lax.psum((col_part, local_loss), "fsdp")
    col_lse = sim_scale + jnp.log(col_total)
    loss = (loss_total + jnp.sum(col_lse)) / (2.0 * npairs)
    d_sims = 0.5 * (jnp.exp(sims - row_lse) + jnp.exp(sims - col_lse[None, :])) - jnp.where(
        matched, 1.0, 0.0
    )
    d_sims_low = (d_sims * sim_scale).astype(jnp.bfloat16)
    d_source = project(d_sims_low, all_targets)
    target_part = weight_grad(d_sims_low, own_sources)
    d_target = lax.psum_scatter(target_part, "fsdp", scatter_dimension=0, tiled=True)
    d_unit = jnp.stack([d_source, d_target], axis=1).reshape(count, D)
    (d_cls,) = pool_back(d_unit)
    d_block = out_cotangent.astype(jnp.float32).at[:, 0, :].add(d_cls).reshape(count * LEN, D)
    inner_back, outer_back, ffn_gain_back = (
        lax.all_gather(w_inner, "fsdp", axis=0, tiled=True),
        lax.all_gather(w_outer, "fsdp", axis=0, tiled=True),
        lax.all_gather(gain_ffn, "fsdp", axis=0, tiled=True),
    )
    _, ffn_norm_back = jax.vjp(scaled_norm, resid_ffn, ffn_gain_back.astype(jnp.float32))
    d_resid_ffn, d_ffn_gain = ffn_norm_back(d_block)
    d_ffn_shift = jnp.sum(d_block, axis=0)
    d_branch = d_resid_ffn.astype(jnp.bfloat16)
    d_outer_bias = column_sum(d_branch)
    d_outer_mat = weight_grad(hidden_act, d_branch)
    d_act = project_back(d_branch, outer_back)
    _, gelu_back = jax.vjp(exact_gelu, hidden_pre)
    (d_pre,) = gelu_back(d_act)
    d_hidden = d_pre.astype(jnp.bfloat16)
    d_inner_mat = weight_grad(normed_low, d_hidden)
    d_inner_bias = column_sum(d_hidden)
    d_normed = d_resid_ffn + project_back(d_hidden, inner_back)
    grad_w_inner, grad_b_inner, grad_w_outer, grad_b_outer, grad_gain_ffn, grad_shift_ffn = (
        lax.psum_scatter(d_inner_mat, "fsdp", scatter_dimension=0, tiled=True),
        lax.psum_scatter(d_inner_bias, "fsdp", scatter_dimension=0, tiled=True),
        lax.psum_scatter(d_outer_mat, "fsdp", scatter_dimension=0, tiled=True),
        lax.psum_scatter(d_outer_bias, "fsdp", scatter_dimension=0, tiled=True),
        lax.psum_scatter(d_ffn_gain, "fsdp", scatter_dimension=0, tiled=True),
        lax.psum_scatter(d_ffn_shift, "fsdp", scatter_dimension=0, tiled=True),
    )
    query_back, key_back, value_back, output_back, attn_gain_back = (
        lax.all_gather(w_query, "fsdp", axis=0, tiled=True),
        lax.all_gather(w_key, "fsdp", axis=0, tiled=True),
        lax.all_gather(w_value, "fsdp", axis=0, tiled=True),
        lax.all_gather(w_output, "fsdp", axis=0, tiled=True),
        lax.all_gather(gain_attn, "fsdp", axis=0, tiled=True),
    )
    _, attn_norm_back = jax.vjp(scaled_norm, resid_attn, attn_gain_back.astype(jnp.float32))
    d_resid_attn, d_attn_gain = attn_norm_back(d_normed)
    d_attn_shift = jnp.sum(d_normed, axis=0)
    d_attn_out = d_resid_attn.astype(jnp.bfloat16)
    d_output_bias = column_sum(d_attn_out)
    d_output_mat = weight_grad(context, d_attn_out)
    d_context = project_back(d_attn_out, output_back).astype(jnp.bfloat16).reshape(shape_four)
    probs_again = jnp.exp(scores_of(queries, key_rows, visible) - score_lse)
    d_probs = jnp.einsum(
        "bqhd,bkhd->bhqk", d_context, value_rows, preferred_element_type=jnp.float32
    )
    d_values = jnp.einsum(
        "bhqk,bqhd->bkhd",
        probs_again.astype(jnp.bfloat16),
        d_context,
        preferred_element_type=jnp.float32,
    )
    d_values = d_values.astype(jnp.bfloat16).reshape(count * LEN, D)
    d_scores = (
        probs_again * (d_probs - jnp.sum(probs_again * d_probs, axis=-1, keepdims=True))
    ).astype(jnp.bfloat16)
    d_queries = jnp.einsum(
        "bhqk,bkhd->bqhd", d_scores, key_rows, preferred_element_type=jnp.float32
    ) * HEAD_DIM ** (-0.5)
    d_queries = d_queries.astype(jnp.bfloat16).reshape(count * LEN, D)
    d_keys = jnp.einsum(
        "bhqk,bqhd->bkhd", d_scores, queries, preferred_element_type=jnp.float32
    ) * HEAD_DIM ** (-0.5)
    d_keys = d_keys.astype(jnp.bfloat16).reshape(count * LEN, D)
    d_query_mat = weight_grad(token_rows, d_queries)
    d_key_mat = weight_grad(token_rows, d_keys)
    d_value_mat = weight_grad(token_rows, d_values)
    d_query_bias = column_sum(d_queries)
    d_value_bias = column_sum(d_values)
    grad_rows = (
        d_resid_attn
        + project_back(d_queries, query_back)
        + project_back(d_keys, key_back)
        + project_back(d_values, value_back)
    )
    (
        grad_w_query,
        grad_w_key,
        grad_w_value,
        grad_w_output,
        grad_b_query,
        grad_b_value,
        grad_b_output,
        grad_gain_attn,
        grad_shift_attn,
    ) = (
        lax.psum_scatter(d_query_mat, "fsdp", scatter_dimension=0, tiled=True),
        lax.psum_scatter(d_key_mat, "fsdp", scatter_dimension=0, tiled=True),
        lax.psum_scatter(d_value_mat, "fsdp", scatter_dimension=0, tiled=True),
        lax.psum_scatter(d_output_mat, "fsdp", scatter_dimension=0, tiled=True),
        lax.psum_scatter(d_query_bias, "fsdp", scatter_dimension=0, tiled=True),
        lax.psum_scatter(d_value_bias, "fsdp", scatter_dimension=0, tiled=True),
        lax.psum_scatter(d_output_bias, "fsdp", scatter_dimension=0, tiled=True),
        lax.psum_scatter(d_attn_gain, "fsdp", scatter_dimension=0, tiled=True),
        lax.psum_scatter(d_attn_shift, "fsdp", scatter_dimension=0, tiled=True),
    )
    return (
        loss,
        block_out,
        grad_rows.reshape(count, LEN, D),
        grad_w_query,
        grad_w_key,
        grad_w_value,
        grad_w_output,
        grad_b_query,
        grad_b_value,
        grad_b_output,
        grad_gain_attn,
        grad_shift_attn,
        grad_w_inner,
        grad_b_inner,
        grad_w_outer,
        grad_b_outer,
        grad_gain_ffn,
        grad_shift_ffn,
    )


def solution(mesh):
    in_specs = (
        P("fsdp", None, None),
        P("fsdp"),
        P("fsdp"),
        P("fsdp", None, None),
        P("fsdp", None),
        P("fsdp", None),
        P("fsdp", None),
        P("fsdp", None),
        P("fsdp"),
        P("fsdp"),
        P("fsdp"),
        P("fsdp"),
        P("fsdp"),
        P("fsdp", None),
        P("fsdp"),
        P("fsdp", None),
        P("fsdp"),
        P("fsdp"),
        P("fsdp"),
    )
    out_specs = (
        P(),
        P("fsdp", None, None),
        P("fsdp", None, None),
        P("fsdp", None),
        P("fsdp", None),
        P("fsdp", None),
        P("fsdp", None),
        P("fsdp"),
        P("fsdp"),
        P("fsdp"),
        P("fsdp"),
        P("fsdp"),
        P("fsdp", None),
        P("fsdp"),
        P("fsdp", None),
        P("fsdp"),
        P("fsdp"),
        P("fsdp"),
    )
    return jax.shard_map(local, mesh=mesh, in_specs=in_specs, out_specs=out_specs, check_vma=False)
```

profile of v0, /device:TPU:0, one launch (start us, length us, event | category | flops | bytes accessed | tf_op | source)
XLA Modules:
  0.0 1316.2 jit_solution(8292508203558177508)
XLA Ops:
  19.5 42.6 %all-reduce.19 = (bf16[768]{0:T(1024)(128)(2,1)S(1)}, bf16[768]{0:T(1024)(128)(2,1)S(1)}, bf16[768]{0:T(1024)(128)(2,1)S(1)}, bf16[768]{0:T(1024)(128)(2,1)S(1)}...) all-reduce(bf16[768]{0:T(1024)(128)(2,1)S(1)} %dynamic-update-slice, ...), channel_id=1, replica_groups=mesh['fsdp'=32] {'fsdp'}, use_global_device_ids=true, to_apply=%add.1 | all-reduce | flops 9216 | bytes 36864
  74.8 48.9 %all-gather.7.cloned.1.call-done = bf16[768,768]{1,0:T(8,128)(2,1)} async-done(((bf16[24,768]{1,0:T(8,128)(2,1)}), bf16[768,768]{1,0:T(8,128)(2,1)}) %all-gather.7.cloned.1.call-update) | async-done | bytes 1179664 | tf_op jit(solution)/shard_map/all_gather | solution.py:85
  130.2 49.4 %all-gather.9.cloned.1.call-done = bf16[768,768]{1,0:T(8,128)(2,1)} async-done(((bf16[24,768]{1,0:T(8,128)(2,1)}), bf16[768,768]{1,0:T(8,128)(2,1)}) %all-gather.9.cloned.1.call-update) | async-done | bytes 1179664 | tf_op jit(solution)/shard_map/all_gather | solution.py:83
  209.9 25.5 %all-gather.13.cloned.1.call-done = bf16[768,768]{1,0:T(8,128)(2,1)} async-done(((bf16[24,768]{1,0:T(8,128)(2,1)}), bf16[768,768]{1,0:T(8,128)(2,1)}) %all-gather.13.cloned.1.call-update) | async-done | bytes 1179664 | tf_op jit(solution)/shard_map/all_gather | solution.py:86
  239.8 61.0 %all-gather.15.cloned.1.call-done = bf16[768,3072]{1,0:T(8,128)(2,1)} async-done(((bf16[24,3072]{1,0:T(8,128)(2,1)}), bf16[768,3072]{1,0:T(8,128)(2,1)}) %all-gather.15.cloned.1.call-update) | async-done | bytes 4718608 | tf_op jit(solution)/shard_map/all_gather | solution.py:125
  300.8 35.8 %multiply_convert_fusion = (bf16[1024,3072]{1,0:T(8,128)(2,1)}, f32[1024,3072]{1,0:T(8,128)}, f32[1024,3072]{1,0:T(8,128)}) fusion(f32[3072]{0:T(1024)S(1)} %convert_element_type.137, bf16[768,3072]{1,0:T(8,128)(2,1)} %all-gather.15.cloned.1.call-done, f32[1024,768]{1,0:T(8,128)S(1)} %get-tuple-element.132, f32[768]{0:T(1024)S(1)} %convert_element_type.135, ...), kind=kOutput, calls=%fused_computation.4 | convolution fusion | flops 5043388416 | bytes 39348224 | tf_op jit(solution)/shard_map/dot_general | solution.py:17
  336.6 29.4 %all-gather.17.cloned.1.call-done = bf16[3072,768]{1,0:T(8,128)(2,1)} async-done(((bf16[96,768]{1,0:T(8,128)(2,1)}), bf16[3072,768]{1,0:T(8,128)(2,1)}) %all-gather.17.cloned.1.call-update) | async-done | bytes 4718608 | tf_op jit(solution)/shard_map/all_gather | solution.py:127
  366.0 9.5 fusion.52
  381.4 44.2 %all_gather.71 = bf16[512,768]{1,0:T(8,128)(2,1)} all-gather(bf16[16,768]{1,0:T(8,128)(2,1)S(1)} %fusion.29), channel_id=1, replica_groups=mesh['fsdp'=32] {'fsdp'}, dimensions={0}, use_global_device_ids=true | all-gather | bytes 811008 | tf_op jit(solution)/shard_map/all_gather | solution.py:142
  432.5 36.8 %psum.15 = f32[256]{0:T(256)S(1)} all-reduce(f32[256]{0:T(256)S(1)} %get-tuple-element.89), channel_id=1, replica_groups=mesh['fsdp'=32] {'fsdp'}, use_global_device_ids=true, to_apply=%region_13.14 | all-reduce | flops 256 | bytes 2048 | tf_op jit(solution)/shard_map/psum | solution.py:156
  476.1 91.7 %reduce-scatter.14.cloned.1.call-done = f32[8,768]{1,0:T(8,128)} async-done(((f32[256,768]{1,0:T(8,128)}), f32[8,768]{1,0:T(8,128)}) %reduce-scatter.14.cloned.1.call-update) | async-done | bytes 24592 | tf_op jit(solution)/shard_map/reduce_scatter | solution.py:165
  578.9 18.3 %convert_reduce_fusion = (f32[3072]{0:T(1024)S(1)}, bf16[1024,3072]{1,0:T(8,128)(2,1)}) fusion(f32[1024,3072]{1,0:T(8,128)} %get-tuple-element.126, bf16[1024,768]{1,0:T(8,128)(2,1)} %get-tuple-element.114, bf16[3072,768]{1,0:T(8,128)(2,1)} %all-gather.17.cloned.1.call-done, f32[1024,3072]{1,0:T(8,128)} %get-tuple-element.133, ...), kind=kOutput, calls=%fused_computation.2 | convolution fusion | flops 4885312512 | bytes 37773312 | tf_op jit(solution)/shard_map/dot_general | solution.py:21
  597.3 9.6 multiply_reduce_fusion.1
  616.5 6.5 reshape.306
  623.0 10.5 multiply_reduce_fusion
  677.6 7.7 convert_reduce_fusion.1
  700.7 10.7 fusion.40
  712.8 10.4 fusion.57
  725.5 40.7 %all-reduce.18 = (f32[]{:T(128)}, f32[768]{0:T(1024)S(1)}, f32[768]{0:T(1024)S(1)}, f32[768]{0:T(1024)S(1)}, f32[768]{0:T(1024)S(1)}, /*index=5*/f32[768]{0:T(10...) all-reduce(f32[]{:T(128)S(6)} %sub.93, ...), channel_id=1, replica_groups=mesh['fsdp'=32] {'fsdp'}, use_global_device_ids=true, to_apply=%region_11.12 | all-reduce | flops 9217 | bytes 73736 | tf_op jit(solution)/shard_map/psum | solution.py:156
  782.5 34.2 %reduce-scatter.24.cloned.1.call-done = f32[24,768]{1,0:T(8,128)} async-done(((f32[768,768]{1,0:T(8,128)}), f32[24,768]{1,0:T(8,128)}) %reduce-scatter.24.cloned.1.call-update) | async-done | bytes 73744
  816.7 103.8 %reduce-scatter.22.cloned.1.call-done = f32[24,768]{1,0:T(8,128)} async-done(((f32[768,768]{1,0:T(8,128)}), f32[24,768]{1,0:T(8,128)}) %reduce-scatter.22.cloned.1.call-update) | async-done | bytes 73744
  920.6 104.8 %reduce-scatter.26.cloned.1.call-done = f32[24,768]{1,0:T(8,128)} async-done(((f32[768,768]{1,0:T(8,128)}), f32[24,768]{1,0:T(8,128)}) %reduce-scatter.26.cloned.1.call-update) | async-done | bytes 73744
  1025.3 140.8 %reduce-scatter.18.cloned.1.call-done = f32[24,3072]{1,0:T(8,128)} async-done(((f32[768,3072]{1,0:T(8,128)}), f32[24,3072]{1,0:T(8,128)}) %reduce-scatter.18.cloned.1.call-update) | async-done | bytes 294928 | tf_op jit(solution)/shard_map/reduce_scatter | solution.py:188
  1166.2 142.1 %reduce-scatter.20.cloned.1.call-done = f32[96,768]{1,0:T(8,128)} async-done(((f32[3072,768]{1,0:T(8,128)}), f32[96,768]{1,0:T(8,128)}) %reduce-scatter.20.cloned.1.call-update) | async-done | bytes 294928 | tf_op jit(solution)/shard_map/reduce_scatter | solution.py:190
  (210 shorter events, 182.4 us)
Async XLA Ops:
  7.2 60.6 %all-gather.11.cloned.1.call-start = ((), (), s32[]{:S(2)}) async-start(), calls=%async_computation.9 | async-start | bytes 1216512 | tf_op jit(solution)/shard_map/all_gather | solution.py:84
  7.9 115.8 %all-gather.7.cloned.1.call-start = ((), (), s32[]{:S(2)}) async-start(), calls=%async_computation.7 | async-start | bytes 1216512 | tf_op jit(solution)/shard_map/all_gather | solution.py:85
  8.7 171.0 %all-gather.9.cloned.1.call-start = ((), (), s32[]{:S(2)}) async-start(), calls=%async_computation.8 | async-start | bytes 1216512 | tf_op jit(solution)/shard_map/all_gather | solution.py:83
  9.4 226.0 %all-gather.13.cloned.1.call-start = ((), (), s32[]{:S(2)}) async-start(), calls=%async_computation.10 | async-start | bytes 1216512 | tf_op jit(solution)/shard_map/all_gather | solution.py:86
  10.0 290.8 %all-gather.15.cloned.1.call-start = ((), (), s32[]{:S(2)}) async-start(), calls=%async_computation.11 | async-start | bytes 4866048 | tf_op jit(solution)/shard_map/all_gather | solution.py:125
  10.6 355.4 %all-gather.17.cloned.1.call-start = ((), (), s32[]{:S(2)}) async-start(), calls=%async_computation.12 | async-start | bytes 4866048 | tf_op jit(solution)/shard_map/all_gather | solution.py:127
  11.1 556.6 %reduce-scatter.14.cloned.1.call-start = ((), (), s32[]{:S(2)}) async-start(), calls=%async_computation.13 | async-start | bytes 811008 | tf_op jit(solution)/shard_map/reduce_scatter | solution.py:165
  70.9 52.8 %copy-start.28 = (bf16[16,64,768]{2,1,0:T(8,128)(2,1)S(1)}, bf16[16,64,768]{2,1,0:T(8,128)(2,1)}, u32[]{:S(2)}) copy-start(bf16[16,64,768]{2,1,0:T(8,128)(2,1)} %param.21) | copy-start | bytes 4718596
  192.6 4.7 copy-start.5
  239.2 97.3 %copy-start.1 = (f32[1024,768]{1,0:T(8,128)}, f32[1024,768]{1,0:T(8,128)S(1)}, u32[]{:S(2)}) copy-start(f32[1024,768]{1,0:T(8,128)S(1)} %get-tuple-element.132) | copy-start | bytes 9437188
  239.8 96.8 %copy-start.25 = (f32[1024]{0:T(1024)}, f32[1024]{0:T(1024)S(1)}, u32[]{:S(2)}) copy-start(f32[1024]{0:T(1024)S(1)} %multiply_reduce_fusion.5) | copy-start | bytes 12292
  378.8 52.6 %copy-start.27 = (s32[8]{0:T(128)S(1)}, s32[8]{0:T(128)}, u32[]{:S(2)}) copy-start(s32[8]{0:T(128)} %param.23) | copy-start | bytes 100
  471.8 310.7 %reduce-scatter.16.cloned.1.call-start = ((), (), s32[]{:S(2)}) async-start(), calls=%async_computation.14 | async-start | bytes 2433024 | tf_op jit(solution)/shard_map/reduce_scatter | solution.py:256
  578.9 18.3 %copy-start.2 = (f32[1024,768]{1,0:T(8,128)S(1)}, f32[1024,768]{1,0:T(8,128)}, u32[]{:S(2)}) copy-start(f32[1024,768]{1,0:T(8,128)} %copy-done.1) | copy-start | bytes 9437188
  578.9 18.3 %copy-start.11 = (f32[1024,768]{1,0:T(8,128)S(1)}, f32[1024,768]{1,0:T(8,128)}, u32[]{:S(2)}) copy-start(f32[1024,768]{1,0:T(8,128)} %copy-done.10) | copy-start | bytes 9437188
  597.2 9.6 copy-start.26
  613.8 202.9 %reduce-scatter.24.cloned.1.call-start = ((), (), s32[]{:S(2)}) async-start(), calls=%async_computation.18 | async-start | bytes 2433024
  616.5 17.0 %slice-start = ((s8[6291456]{0:T(1024)(128)(4,1)}), s8[2097152]{0:T(1024)(128)(4,1)S(1)}, s32[]{:S(2)}) async-start(s8[6291456]{0:T(1024)(128)(4,1)} %bitcast.113), calls=%async_computation.20 | async-start | bytes 4194304
  623.0 10.6 slice-start.1
  633.5 6.6 copy-start.6
  658.9 261.6 %reduce-scatter.22.cloned.1.call-start = ((), (), s32[]{:S(2)}) async-start(), calls=%async_computation.17 | async-start | bytes 2433024
  677.6 347.8 %reduce-scatter.26.cloned.1.call-start = ((), (), s32[]{:S(2)}) async-start(), calls=%async_computation.19 | async-start | bytes 2433024
  700.6 465.5 %reduce-scatter.18.cloned.1.call-start = ((), (), s32[]{:S(2)}) async-start(), calls=%async_computation.15 | async-start | bytes 9732096 | tf_op jit(solution)/shard_map/reduce_scatter | solution.py:188
  711.4 596.9 %reduce-scatter.20.cloned.1.call-start = ((), (), s32[]{:S(2)}) async-start(), calls=%async_computation.16 | async-start | bytes 9732096 | tf_op jit(solution)/shard_map/reduce_scatter | solution.py:190
  (22 other events, 58.8 us)
Sparse Core Ops, SparseCore 0:
  10.9 56.8 all-gather.10
  70.7 53.0 all-gather.6
  126.6 52.9 all-gather.8
  182.4 52.9 all-gather.12
  238.1 62.5 all-gather.14
  303.5 62.4 all-gather.16
  471.9 95.8 reduce-scatter.13
  613.9 98.0 reduce-scatter.15
  718.7 97.9 reduce-scatter.23
  822.4 98.0 reduce-scatter.21
  927.3 98.0 reduce-scatter.25
  1031.7 134.4 reduce-scatter.17
  1173.6 134.5 reduce-scatter.19
where the time goes:
time: 1330 us; the launch traced here: 1320 us
  waiting for transfers between devices  841 us (63%)
  matrix products  169 us (13%)
  blocking collectives  164 us (12%)
  local copies, waits for them, and re-layouts  95.5 us (7%)
  other arithmetic  26.6 us (2%)
  between operations  18.8 us (1%)
    unnamed x16, waiting for transfers between devices  247 us
    reduce_scatter x1, waiting for transfers between devices, local(): lax.psum_scatter(d_outer_mat, 'fsdp', scatter_dimension=0, tiled=True)  142 us
    reduce_scatter x1, waiting for transfers between devices, local(): lax.psum_scatter(d_inner_mat, 'fsdp', scatter_dimension=0, tiled=True)  141 us
    reduce_scatter x1, waiting for transfers between devices, local(): lax.psum_scatter(target_part, 'fsdp', scatter_dimension=0, tiled=True)  91.7 us
    psum x2, blocking collectives, local(): col_total, loss_total = lax.psum((col_part, local_loss), 'fsdp')  77.6 us
    all_gather x1, waiting for transfers between devices, local(): lax.all_gather(w_inner, 'fsdp', axis=0, tiled=True)  61 us
    dot_general x7, matrix products, project(): return jnp.dot(rows, weight, preferred_element_type=jnp.float32)  57.8 us
    all_gather x1, waiting for transfers between devices, local(): lax.all_gather(w_query, 'fsdp', axis=0, tiled=True)  49.4 us
  transfers between devices with their start and end apart: 13, of which 12 were waited for; matrix products, arithmetic and copies ran while one was open for 16% of the time, Pallas kernels for 0%

commit v1 on v0

--- a/solution.py
+++ b/solution.py
@@ -11,6 +11,28 @@
 pool_eps = 1e-06
 sim_scale = 50.0
 sim_margin = 0.3
+
+
+def joined_along(blocks, dim):
+    shape = list(blocks.shape[1:])
+    shape[dim] *= blocks.shape[0]
+    return jnp.moveaxis(blocks, 0, dim).reshape(shape)
+
+
+def grow_blocks(array, axis):
+    size = lax.axis_size(axis)
+    blocks = array[None]
+    for level in range(size.bit_length() - 1):
+        stride = 1 << level
+        other = lax.ppermute(blocks, axis, [(i, i ^ stride) for i in range(size)])
+        both = jnp.stack([blocks, other])
+        upper = lax.axis_index(axis) >> level & 1
+        blocks = jnp.where(upper == 0, both, both[::-1]).reshape(-1, *array.shape)
+    return blocks
+
+
+def doubled_up(value, axis, dim):
+    return joined_along(grow_blocks(value, axis), dim)
 
 
 def project(rows, weight):
@@ -139,7 +161,7 @@
     cls_rows = block_rows.reshape(count, LEN, D)[:, 0, :]
     unit, pool_back = jax.vjp(normalize, cls_rows)
     unit_low = unit.astype(jnp.bfloat16)
-    every_unit = lax.all_gather(unit_low, "fsdp", axis=0, tiled=True)
+    every_unit = doubled_up(unit_low, "fsdp", 0)
     every_pair = every_unit.reshape(every_unit.shape[0] // 2, 2, D)
     all_targets = every_pair[:, 1, :]
     own_pair = unit_low.reshape(half, 2, D)

time: 1330 us -> 1320 us (level)
  blocking collectives: 164 us -> 121 us
  waiting for transfers between devices: 841 us -> 868 us
    all_gather x1 -> x0, blocking collectives: 44.2 us -> none  [local(): every_unit = lax.all_gather(unit_low, 'fsdp', axis=0, tiled=True)]
    ppermute x0 -> x5, waiting for transfers between devices: none -> 25.8 us  [grow_blocks(): other = lax.ppermute(blocks, axis, [(i, i ^ stride) for i in range(size)])]
  transfers between devices with their start and end apart: 13 -> 18, of which waited for: 12 -> 17; matrix products, arithmetic and copies ran while one was open for 16% -> 16% of each run, Pallas kernels for 0% -> 0%
where the time goes in v1:
time: 1320 us; the launch traced here: 1310 us
  waiting for transfers between devices  868 us (66%)
  matrix products  169 us (13%)
  blocking collectives  121 us (9%)
  local copies, waits for them, and re-layouts  95.6 us (7%)
  other arithmetic  30.9 us (2%)
  between operations  18.9 us (1%)
    unnamed x16, waiting for transfers between devices  246 us
    reduce_scatter x1, waiting for transfers between devices, local(): lax.psum_scatter(d_outer_mat, 'fsdp', scatter_dimension=0, tiled=True)  142 us
    reduce_scatter x1, waiting for transfers between devices, local(): lax.psum_scatter(d_inner_mat, 'fsdp', scatter_dimension=0, tiled=True)  141 us
    reduce_scatter x1, waiting for transfers between devices, local(): lax.psum_scatter(target_part, 'fsdp', scatter_dimension=0, tiled=True)  92.7 us
    psum x2, blocking collectives, local(): col_total, loss_total = lax.psum((col_part, local_loss), 'fsdp')  78.2 us
    all_gather x1, waiting for transfers between devices, local(): lax.all_gather(w_inner, 'fsdp', axis=0, tiled=True)  61 us
    dot_general x7, matrix products, project(): return jnp.dot(rows, weight, preferred_element_type=jnp.float32)  57.7 us
    all_gather x1, waiting for transfers between devices, local(): lax.all_gather(w_query, 'fsdp', axis=0, tiled=True)  49.4 us
  transfers between devices with their start and end apart: 18, of which 17 were waited for; matrix products, arithmetic and copies ran while one was open for 16% of the time, Pallas kernels for 0%

profile of v1, /device:TPU:0, one launch (start us, length us, event | category | flops | bytes accessed | tf_op | source)
XLA Modules:
  0.0 1311.0 jit_solution(8403193185703098504)
XLA Ops:
  19.5 42.6 %all-reduce.19 = (bf16[768]{0:T(1024)(128)(2,1)S(1)}, bf16[768]{0:T(1024)(128)(2,1)S(1)}, bf16[768]{0:T(1024)(128)(2,1)S(1)}, bf16[768]{0:T(1024)(128)(2,1)S(1)}...) all-reduce(bf16[768]{0:T(1024)(128)(2,1)S(1)} %dynamic-update-slice, ...), channel_id=1, replica_groups=mesh['fsdp'=32] {'fsdp'}, use_global_device_ids=true, to_apply=%add.1 | all-reduce | flops 9216 | bytes 36864
  74.8 48.9 %all-gather.7.cloned.1.call-done = bf16[768,768]{1,0:T(8,128)(2,1)} async-done(((bf16[24,768]{1,0:T(8,128)(2,1)}), bf16[768,768]{1,0:T(8,128)(2,1)}) %all-gather.7.cloned.1.call-update) | async-done | bytes 1179664 | tf_op jit(solution)/shard_map/all_gather | solution.py:107
  130.2 49.4 %all-gather.9.cloned.1.call-done = bf16[768,768]{1,0:T(8,128)(2,1)} async-done(((bf16[24,768]{1,0:T(8,128)(2,1)}), bf16[768,768]{1,0:T(8,128)(2,1)}) %all-gather.9.cloned.1.call-update) | async-done | bytes 1179664 | tf_op jit(solution)/shard_map/all_gather | solution.py:105
  209.9 25.5 %all-gather.13.cloned.1.call-done = bf16[768,768]{1,0:T(8,128)(2,1)} async-done(((bf16[24,768]{1,0:T(8,128)(2,1)}), bf16[768,768]{1,0:T(8,128)(2,1)}) %all-gather.13.cloned.1.call-update) | async-done | bytes 1179664 | tf_op jit(solution)/shard_map/all_gather | solution.py:108
  239.8 61.0 %all-gather.15.cloned.1.call-done = bf16[768,3072]{1,0:T(8,128)(2,1)} async-done(((bf16[24,3072]{1,0:T(8,128)(2,1)}), bf16[768,3072]{1,0:T(8,128)(2,1)}) %all-gather.15.cloned.1.call-update) | async-done | bytes 4718608 | tf_op jit(solution)/shard_map/all_gather | solution.py:147
  300.8 35.8 %multiply_convert_fusion = (bf16[1024,3072]{1,0:T(8,128)(2,1)}, f32[1024,3072]{1,0:T(8,128)}, f32[1024,3072]{1,0:T(8,128)}) fusion(f32[3072]{0:T(1024)S(1)} %convert_element_type.153, bf16[768,3072]{1,0:T(8,128)(2,1)} %all-gather.15.cloned.1.call-done, f32[1024,768]{1,0:T(8,128)S(1)} %get-tuple-element.152, f32[768]{0:T(1024)S(1)} %convert_element_type.151, ...), kind=kOutput, calls=%fused_computation.4 | convolution fusion | flops 5043388416 | bytes 39348224 | tf_op jit(solution)/shard_map/dot_general | solution.py:39
  336.5 29.4 %all-gather.17.cloned.1.call-done = bf16[3072,768]{1,0:T(8,128)(2,1)} async-done(((bf16[96,768]{1,0:T(8,128)(2,1)}), bf16[3072,768]{1,0:T(8,128)(2,1)}) %all-gather.17.cloned.1.call-update) | async-done | bytes 4718608 | tf_op jit(solution)/shard_map/all_gather | solution.py:149
  366.0 9.5 fusion.59
  401.4 15.3 %collective-permute-done.4 = bf16[16,16,768]{2,1,0:T(8,128)(2,1)} collective-permute-done((bf16[16,16,768]{2,1,0:T(8,128)(2,1)}, bf16[16,16,768]{2,1,0:T(8,128)(2,1)}, u32[]{:S(2)}, u32[]{:S(2)}) %collective-permute-start.4) | collective-permute-done | bytes 393248 | tf_op jit(solution)/shard_map/ppermute | solution.py:27
  425.8 37.3 %psum.15 = f32[256]{0:T(256)S(1)} all-reduce(f32[256]{0:T(256)S(1)} %get-tuple-element.107), channel_id=1, replica_groups=mesh['fsdp'=32] {'fsdp'}, use_global_device_ids=true, to_apply=%region_13.14 | all-reduce | flops 256 | bytes 2048 | tf_op jit(solution)/shard_map/psum | solution.py:178
  469.9 92.7 %reduce-scatter.14.cloned.1.call-done = f32[8,768]{1,0:T(8,128)} async-done(((f32[256,768]{1,0:T(8,128)}), f32[8,768]{1,0:T(8,128)}) %reduce-scatter.14.cloned.1.call-update) | async-done | bytes 24592 | tf_op jit(solution)/shard_map/reduce_scatter | solution.py:187
  573.7 18.3 %convert_reduce_fusion = (f32[3072]{0:T(1024)S(1)}, bf16[1024,3072]{1,0:T(8,128)(2,1)}) fusion(f32[1024,3072]{1,0:T(8,128)} %get-tuple-element.144, bf16[1024,768]{1,0:T(8,128)(2,1)} %get-tuple-element.132, bf16[3072,768]{1,0:T(8,128)(2,1)} %all-gather.17.cloned.1.call-done, f32[1024,3072]{1,0:T(8,128)} %get-tuple-element.153, ...), kind=kOutput, calls=%fused_computation.2 | convolution fusion | flops 4885312512 | bytes 37773312 | tf_op jit(solution)/shard_map/dot_general | solution.py:43
  592.0 9.6 multiply_reduce_fusion.1
  611.2 6.5 reshape.382
  617.7 10.5 multiply_reduce_fusion
  672.4 7.7 convert_reduce_fusion.1
  695.4 10.6 fusion.47
  707.5 10.4 fusion.64
  720.2 40.9 %all-reduce.18 = (f32[]{:T(128)}, f32[768]{0:T(1024)S(1)}, f32[768]{0:T(1024)S(1)}, f32[768]{0:T(1024)S(1)}, f32[768]{0:T(1024)S(1)}, /*index=5*/f32[768]{0:T(10...) all-reduce(f32[]{:T(128)S(6)} %sub.93, ...), channel_id=1, replica_groups=mesh['fsdp'=32] {'fsdp'}, use_global_device_ids=true, to_apply=%region_11.12 | all-reduce | flops 9217 | bytes 73736 | tf_op jit(solution)/shard_map/psum | solution.py:178
  777.4 34.2 %reduce-scatter.24.cloned.1.call-done = f32[24,768]{1,0:T(8,128)} async-done(((f32[768,768]{1,0:T(8,128)}), f32[24,768]{1,0:T(8,128)}) %reduce-scatter.24.cloned.1.call-update) | async-done | bytes 73744
  811.6 103.7 %reduce-scatter.22.cloned.1.call-done = f32[24,768]{1,0:T(8,128)} async-done(((f32[768,768]{1,0:T(8,128)}), f32[24,768]{1,0:T(8,128)}) %reduce-scatter.22.cloned.1.call-update) | async-done | bytes 73744
  915.3 104.8 %reduce-scatter.26.cloned.1.call-done = f32[24,768]{1,0:T(8,128)} async-done(((f32[768,768]{1,0:T(8,128)}), f32[24,768]{1,0:T(8,128)}) %reduce-scatter.26.cloned.1.call-update) | async-done | bytes 73744
  1020.1 140.9 %reduce-scatter.18.cloned.1.call-done = f32[24,3072]{1,0:T(8,128)} async-done(((f32[768,3072]{1,0:T(8,128)}), f32[24,3072]{1,0:T(8,128)}) %reduce-scatter.18.cloned.1.call-update) | async-done | bytes 294928 | tf_op jit(solution)/shard_map/reduce_scatter | solution.py:210
  1161.0 142.1 %reduce-scatter.20.cloned.1.call-done = f32[96,768]{1,0:T(8,128)} async-done(((f32[3072,768]{1,0:T(8,128)}), f32[96,768]{1,0:T(8,128)}) %reduce-scatter.20.cloned.1.call-update) | async-done | bytes 294928 | tf_op jit(solution)/shard_map/reduce_scatter | solution.py:212
  (230 shorter events, 204.6 us)
Async XLA Ops:
  7.2 60.6 %all-gather.11.cloned.1.call-start = ((), (), s32[]{:S(2)}) async-start(), calls=%async_computation.9 | async-start | bytes 1216512 | tf_op jit(solution)/shard_map/all_gather | solution.py:106
  7.9 115.8 %all-gather.7.cloned.1.call-start = ((), (), s32[]{:S(2)}) async-start(), calls=%async_computation.7 | async-start | bytes 1216512 | tf_op jit(solution)/shard_map/all_gather | solution.py:107
  8.7 171.0 %all-gather.9.cloned.1.call-start = ((), (), s32[]{:S(2)}) async-start(), calls=%async_computation.8 | async-start | bytes 1216512 | tf_op jit(solution)/shard_map/all_gather | solution.py:105
  9.4 226.0 %all-gather.13.cloned.1.call-start = ((), (), s32[]{:S(2)}) async-start(), calls=%async_computation.10 | async-start | bytes 1216512 | tf_op jit(solution)/shard_map/all_gather | solution.py:108
  10.0 290.8 %all-gather.15.cloned.1.call-start = ((), (), s32[]{:S(2)}) async-start(), calls=%async_computation.11 | async-start | bytes 4866048 | tf_op jit(solution)/shard_map/all_gather | solution.py:147
  10.6 355.4 %all-gather.17.cloned.1.call-start = ((), (), s32[]{:S(2)}) async-start(), calls=%async_computation.12 | async-start | bytes 4866048 | tf_op jit(solution)/shard_map/all_gather | solution.py:149
  11.1 551.4 %reduce-scatter.14.cloned.1.call-start = ((), (), s32[]{:S(2)}) async-start(), calls=%async_computation.13 | async-start | bytes 811008 | tf_op jit(solution)/shard_map/reduce_scatter | solution.py:187
  70.9 52.8 %copy-start.28 = (bf16[16,64,768]{2,1,0:T(8,128)(2,1)S(1)}, bf16[16,64,768]{2,1,0:T(8,128)(2,1)}, u32[]{:S(2)}) copy-start(bf16[16,64,768]{2,1,0:T(8,128)(2,1)} %param.21) | copy-start | bytes 4718596
  239.2 97.3 %copy-start.1 = (f32[1024,768]{1,0:T(8,128)}, f32[1024,768]{1,0:T(8,128)S(1)}, u32[]{:S(2)}) copy-start(f32[1024,768]{1,0:T(8,128)S(1)} %get-tuple-element.152) | copy-start | bytes 9437188
  239.8 96.8 %copy-start.25 = (f32[1024]{0:T(1024)}, f32[1024]{0:T(1024)S(1)}, u32[]{:S(2)}) copy-start(f32[1024]{0:T(1024)S(1)} %multiply_reduce_fusion.5) | copy-start | bytes 12292
  381.2 1.2 collective-permute-start
  382.5 4.2 collective-permute-start.1
  386.6 4.7 collective-permute-start.2
  391.4 5.8 collective-permute-start.3
  399.0 17.6 %collective-permute-start.4 = (bf16[16,16,768]{2,1,0:T(8,128)(2,1)}, bf16[16,16,768]{2,1,0:T(8,128)(2,1)}, u32[]{:S(2)}, u32[]{:S(2)}) collective-permute-start(bf16[16,16,768]{2,1,0:T(8,128)(2,1)} %bitcast.17), channel_id=1, source_target_pairs={{0,16},{1,17},{2,18},{3,19},{4,20},{5,21},{6,22},{7,23},{8,24},{9,... | collective-permute-start | bytes 1179656 | tf_op jit(solution)/shard_map/ppermute | solution.py:27
  465.5 311.9 %reduce-scatter.16.cloned.1.call-start = ((), (), s32[]{:S(2)}) async-start(), calls=%async_computation.14 | async-start | bytes 2433024 | tf_op jit(solution)/shard_map/reduce_scatter | solution.py:278
  573.7 18.3 %copy-start.2 = (f32[1024,768]{1,0:T(8,128)S(1)}, f32[1024,768]{1,0:T(8,128)}, u32[]{:S(2)}) copy-start(f32[1024,768]{1,0:T(8,128)} %copy-done.1) | copy-start | bytes 9437188
  573.7 18.3 %copy-start.11 = (f32[1024,768]{1,0:T(8,128)S(1)}, f32[1024,768]{1,0:T(8,128)}, u32[]{:S(2)}) copy-start(f32[1024,768]{1,0:T(8,128)} %copy-done.10) | copy-start | bytes 9437188
  608.5 203.0 %reduce-scatter.24.cloned.1.call-start = ((), (), s32[]{:S(2)}) async-start(), calls=%async_computation.18 | async-start | bytes 2433024
  611.2 17.0 %slice-start = ((s8[6291456]{0:T(1024)(128)(4,1)}), s8[2097152]{0:T(1024)(128)(4,1)S(1)}, s32[]{:S(2)}) async-start(s8[6291456]{0:T(1024)(128)(4,1)} %bitcast.136), calls=%async_computation.20 | async-start | bytes 4194304
  653.7 261.6 %reduce-scatter.22.cloned.1.call-start = ((), (), s32[]{:S(2)}) async-start(), calls=%async_computation.17 | async-start | bytes 2433024
  672.3 347.8 %reduce-scatter.26.cloned.1.call-start = ((), (), s32[]{:S(2)}) async-start(), calls=%async_computation.19 | async-start | bytes 2433024
  695.4 465.6 %reduce-scatter.18.cloned.1.call-start = ((), (), s32[]{:S(2)}) async-start(), calls=%async_computation.15 | async-start | bytes 9732096 | tf_op jit(solution)/shard_map/reduce_scatter | solution.py:210
  706.1 597.0 %reduce-scatter.20.cloned.1.call-start = ((), (), s32[]{:S(2)}) async-start(), calls=%async_computation.16 | async-start | bytes 9732096 | tf_op jit(solution)/shard_map/reduce_scatter | solution.py:212
  (27 other events, 98.3 us)
Sparse Core Ops, SparseCore 0:
  10.9 56.8 all-gather.10
  70.7 53.0 all-gather.6
  126.6 52.9 all-gather.8
  182.4 52.9 all-gather.12
  238.1 62.5 all-gather.14
  303.5 62.4 all-gather.16
  465.6 96.8 reduce-scatter.13
  608.7 98.0 reduce-scatter.15
  713.5 98.0 reduce-scatter.23
  817.3 97.9 reduce-scatter.21
  922.0 98.0 reduce-scatter.25
  1026.4 134.5 reduce-scatter.17
  1168.5 134.5 reduce-scatter.19
